TPU v7x, 32 devices: a whole 2x2x4 slice. The times are simulated.
32 devices in a mesh: slab: 8 (over z, y), pencil: 4 (over x, core).
Axes of the slice: x: 2, y: 2, z: 4, core: 2. Of those that a mesh axis runs over, the one named last changes fastest.
Arguments:
- final_adjoint: bfloat16 [32, 128, 1024], P('slab', 'pencil'), may hold values from -6 to 6
- departure: int32 [4, 32, 128], P(None, 'slab', 'pencil'), may hold values from 1 to 29, as said below
- fraction: float32 [4, 32, 128, 1024], P(None, 'slab', 'pencil'), may hold values from 0 to 1
- image: float32 [32, 128, 1024], P('slab', 'pencil'), may hold values from -6 to 6
Outputs:
- adjoint_start: bfloat16 [32, 128, 1024], P('slab', 'pencil')
- body_force: float32 [3, 32, 128, 1024], P(None, 'slab', 'pencil')
Inputs may be any that keep to these rules, and one draw needn't show every extreme that they name: Each base row departure[s][i, j] equals i + d, kept within the volume's range, with an integer displacement d of magnitude at most 4; in every step some blocks have d = 4 and some d = -4.
All inputs are finite; a program needn't handle non-finite values.
Results may differ from a plain program's by a relative error of at most 0.0055.
Values sent between devices are 32-bit elements; how exact they have to be, the bound alone decides.
A program may use at most 64 MiB of HBM per device.

v0:
```python
import jax
import jax.numpy as jnp
from jax import lax
from jax.sharding import PartitionSpec as P


def extended_2(array, sides, width):
    for axis, dim in sides:
        devices, length = (lax.axis_size(axis), array.shape[dim])
        up = [(i, (i + 1) % devices) for i in range(devices - 1)]
        down = [(j, i) for i, j in up]
        last = lax.slice_in_dim(array, length - width, length, axis=dim)
        leading = lax.slice_in_dim(array, 0, width, axis=dim)
        before = lax.ppermute(last, axis, up)
        after = lax.ppermute(leading, axis, down)
        array = jnp.concatenate([before, array, after], axis=dim)
    return array


def from_behind(array, axis, by):
    devices = lax.axis_size(axis)
    pairs = [(i, i + by) for i in range(devices) if 0 <= i + by < devices]
    return lax.ppermute(array, axis, pairs)


def spline_weights(fraction):
    rest = 1.0 - fraction
    square = fraction * fraction
    cube = square * fraction
    return (
        rest * rest * rest / 6.0,
        (3.0 * cube - 6.0 * square + 4.0) / 6.0,
        (-3.0 * cube + 3.0 * square + 3.0 * fraction + 1.0) / 6.0,
        cube / 6.0,
    )


def shards(final_adjoint, departure, fraction, image):
    steps_count = departure.shape[0]
    slab_rows = departure.shape[1]
    columns = departure.shape[2]
    line = image.shape[2]
    blocks = slab_rows * columns
    span = 3 * slab_rows + 3
    places = span * columns
    slab_start = lax.axis_index("slab") * slab_rows
    place_index = jnp.arange(places, dtype=jnp.int32)
    column_of = jnp.tile(jnp.arange(columns, dtype=jnp.int32), slab_rows)
    padded = extended_2(image, (("slab", 0), ("pencil", 1)), 1)
    adjoint = final_adjoint
    for step in reversed(range(steps_count)):
        first_row = departure[step].reshape(blocks) - slab_start + slab_rows
        weights = spline_weights(fraction[step].reshape(blocks, line))
        values = adjoint.reshape(blocks, line).astype(jnp.float32)
        extended = jnp.zeros((places, line), jnp.float32)
        for offset in range(4):
            where_to = (first_row + offset) * columns + column_of
            onehot = (place_index[:, None] == where_to[None, :]).astype(jnp.float32)
            extended = extended + jnp.dot(
                onehot,
                weights[offset] * values,
                precision=lax.Precision.HIGHEST,
                preferred_element_type=jnp.float32,
            )
        extended = extended.reshape(span, columns, line)
        far_lower = extended[0:1]
        near_lower = extended[1 : slab_rows + 1]
        owned = extended[slab_rows + 1 : 2 * slab_rows + 1]
        near_upper = extended[2 * slab_rows + 1 : 3 * slab_rows + 1]
        far_upper = extended[3 * slab_rows + 1 :]
        from_upper = from_behind(near_lower, "slab", -1)
        from_lower = from_behind(near_upper, "slab", 1)
        owned = owned + from_upper + from_lower
        far_from_upper = from_behind(far_lower, "slab", -2)
        far_from_lower = from_behind(far_upper, "slab", 2)
        owned = owned.at[slab_rows - 1 :].add(far_from_upper)
        owned = owned.at[0:2].add(far_from_lower)
        adjoint = owned.astype(jnp.bfloat16)
    along_first = (padded[2:, 1:-1] - padded[:-2, 1:-1]) * 0.5
    along_second = (padded[1:-1, 2:] - padded[1:-1, :-2]) * 0.5
    deep_pad = jnp.pad(image, ((0, 0), (0, 0), (1, 1)))
    along_third = (deep_pad[:, :, 2:] - deep_pad[:, :, :-2]) * 0.5
    weight_field = adjoint.astype(jnp.float32)
    body_force = jnp.stack(
        [weight_field * along_first, weight_field * along_second, weight_field * along_third],
        axis=0,
    )
    return (adjoint, body_force)


def solution(mesh):
    in_specs = (
        P("slab", "pencil", None),
        P(None, "slab", "pencil"),
        P(None, "slab", "pencil", None),
        P("slab", "pencil", None),
    )
    out_specs = (P("slab", "pencil", None), P(None, "slab", "pencil", None))
    return jax.shard_map(shards, mesh=mesh, in_specs=in_specs, out_specs=out_specs, check_vma=False)
```

profile of v0, /device:TPU:20, one launch (start us, length us, event | category | flops | bytes accessed | tf_op | source)
XLA Modules:
  0.0 161.2 jit_solution(10777175245171863272)
XLA Ops:
  10.1 2.4 %collective-permute-start = (f32[4,32,1024]{2,1,0:T(8,128)S(1)}, f32[4,32,1024]{2,1,0:T(8,128)S(1)}, u32[]{:S(2)}, u32[]{:S(2)}) collective-permute-start(f32[4,32,1024]{2,1,0:T(8,128)S(1)} %bitcast.88), channel_id=1, source_target_pairs={{4,0},{8,4},{12,8},{16,12},{20,16},{24,20},{28,24},{5,1},{9,5},{13... | collective-permute-start | bytes 1572872 | tf_op jit(solution)/shard_map/ppermute | solution.py:23
  12.5 4.3 %collective-permute-start.1 = (f32[4,32,1024]{2,1,0:T(8,128)S(1)}, f32[4,32,1024]{2,1,0:T(8,128)S(1)}, u32[]{:S(2)}, u32[]{:S(2)}) collective-permute-start(f32[4,32,1024]{2,1,0:T(8,128)S(1)} %bitcast.85), channel_id=1, source_target_pairs={{0,4},{4,8},{8,12},{12,16},{16,20},{20,24},{24,28},{1,5},{5,9},{9,... | collective-permute-start | bytes 1572872 | tf_op jit(solution)/shard_map/ppermute | solution.py:23
  16.9 2.4 %collective-permute-start.2 = (f32[1,32,1024]{2,1,0:T(8,128)S(1)}, f32[1,32,1024]{2,1,0:T(8,128)S(1)}, u32[]{:S(2)}, u32[]{:S(2)}) collective-permute-start(f32[1,32,1024]{2,1,0:T(8,128)S(1)} %slice_bitcast_fusion.3), channel_id=1, source_target_pairs={{8,0},{12,4},{16,8},{20,12},{24,16},{28,20},{9,1},{13,5},{17,9},{2... | collective-permute-start | bytes 393224 | tf_op jit(solution)/shard_map/ppermute | solution.py:23
  19.3 3.5 %collective-permute-start.3 = (f32[2,32,1024]{2,1,0:T(8,128)S(1)}, f32[2,32,1024]{2,1,0:T(8,128)S(1)}, u32[]{:S(2)}, u32[]{:S(2)}) collective-permute-start(f32[2,32,1024]{2,1,0:T(8,128)S(1)} %bitcast.93), channel_id=1, source_target_pairs={{0,8},{4,12},{8,16},{12,20},{16,24},{20,28},{1,9},{5,13},{9,17},{1... | collective-permute-start | bytes 786440 | tf_op jit(solution)/shard_map/ppermute | solution.py:23
  22.9 12.0 %collective-permute-done = f32[4,32,1024]{2,1,0:T(8,128)S(1)} collective-permute-done((f32[4,32,1024]{2,1,0:T(8,128)S(1)}, f32[4,32,1024]{2,1,0:T(8,128)S(1)}, u32[]{:S(2)}, u32[]{:S(2)}) %collective-permute-start) | collective-permute-done | bytes 524320 | tf_op jit(solution)/shard_map/ppermute | solution.py:23
  34.9 2.9 %collective-permute-done.1 = f32[4,32,1024]{2,1,0:T(8,128)S(1)} collective-permute-done((f32[4,32,1024]{2,1,0:T(8,128)S(1)}, f32[4,32,1024]{2,1,0:T(8,128)S(1)}, u32[]{:S(2)}, u32[]{:S(2)}) %collective-permute-start.1) | collective-permute-done | bytes 524320 | tf_op jit(solution)/shard_map/ppermute | solution.py:23
  42.7 1.9 %collective-permute-start.4 = (f32[4,32,1024]{2,1,0:T(8,128)S(1)}, f32[4,32,1024]{2,1,0:T(8,128)S(1)}, u32[]{:S(2)}, u32[]{:S(2)}) collective-permute-start(f32[4,32,1024]{2,1,0:T(8,128)S(1)} %bitcast.89), channel_id=1, source_target_pairs={{4,0},{8,4},{12,8},{16,12},{20,16},{24,20},{28,24},{5,1},{9,5},{13... | collective-permute-start | bytes 1572872 | tf_op jit(solution)/shard_map/ppermute | solution.py:23
  44.6 4.8 %collective-permute-start.5 = (f32[4,32,1024]{2,1,0:T(8,128)S(1)}, f32[4,32,1024]{2,1,0:T(8,128)S(1)}, u32[]{:S(2)}, u32[]{:S(2)}) collective-permute-start(f32[4,32,1024]{2,1,0:T(8,128)S(1)} %bitcast.86), channel_id=1, source_target_pairs={{0,4},{4,8},{8,12},{12,16},{16,20},{20,24},{24,28},{1,5},{5,9},{9,... | collective-permute-start | bytes 1572872 | tf_op jit(solution)/shard_map/ppermute | solution.py:23
  49.6 2.4 %collective-permute-start.6 = (f32[1,32,1024]{2,1,0:T(8,128)S(1)}, f32[1,32,1024]{2,1,0:T(8,128)S(1)}, u32[]{:S(2)}, u32[]{:S(2)}) collective-permute-start(f32[1,32,1024]{2,1,0:T(8,128)S(1)} %slice_bitcast_fusion.2), channel_id=1, source_target_pairs={{8,0},{12,4},{16,8},{20,12},{24,16},{28,20},{9,1},{13,5},{17,9},{2... | collective-permute-start | bytes 393224 | tf_op jit(solution)/shard_map/ppermute | solution.py:23
  52.0 3.7 %collective-permute-start.7 = (f32[2,32,1024]{2,1,0:T(8,128)S(1)}, f32[2,32,1024]{2,1,0:T(8,128)S(1)}, u32[]{:S(2)}, u32[]{:S(2)}) collective-permute-start(f32[2,32,1024]{2,1,0:T(8,128)S(1)} %bitcast.90), channel_id=1, source_target_pairs={{0,8},{4,12},{8,16},{12,20},{16,24},{20,28},{1,9},{5,13},{9,17},{1... | collective-permute-start | bytes 786440 | tf_op jit(solution)/shard_map/ppermute | solution.py:23
  55.7 11.8 %collective-permute-done.4 = f32[4,32,1024]{2,1,0:T(8,128)S(1)} collective-permute-done((f32[4,32,1024]{2,1,0:T(8,128)S(1)}, f32[4,32,1024]{2,1,0:T(8,128)S(1)}, u32[]{:S(2)}, u32[]{:S(2)}) %collective-permute-start.4) | collective-permute-done | bytes 524320 | tf_op jit(solution)/shard_map/ppermute | solution.py:23
  67.5 3.1 %collective-permute-done.5 = f32[4,32,1024]{2,1,0:T(8,128)S(1)} collective-permute-done((f32[4,32,1024]{2,1,0:T(8,128)S(1)}, f32[4,32,1024]{2,1,0:T(8,128)S(1)}, u32[]{:S(2)}, u32[]{:S(2)}) %collective-permute-start.5) | collective-permute-done | bytes 524320 | tf_op jit(solution)/shard_map/ppermute | solution.py:23
  77.4 4.8 %collective-permute-start.9 = (f32[4,32,1024]{2,1,0:T(8,128)S(1)}, f32[4,32,1024]{2,1,0:T(8,128)S(1)}, u32[]{:S(2)}, u32[]{:S(2)}) collective-permute-start(f32[4,32,1024]{2,1,0:T(8,128)S(1)} %bitcast.84), channel_id=1, source_target_pairs={{0,4},{4,8},{8,12},{12,16},{16,20},{20,24},{24,28},{1,5},{5,9},{9,... | collective-permute-start | bytes 1572872 | tf_op jit(solution)/shard_map/ppermute | solution.py:23
  82.4 2.4 %collective-permute-start.10 = (f32[1,32,1024]{2,1,0:T(8,128)S(1)}, f32[1,32,1024]{2,1,0:T(8,128)S(1)}, u32[]{:S(2)}, u32[]{:S(2)}) collective-permute-start(f32[1,32,1024]{2,1,0:T(8,128)S(1)} %slice_bitcast_fusion.1), channel_id=1, source_target_pairs={{8,0},{12,4},{16,8},{20,12},{24,16},{28,20},{9,1},{13,5},{17,9},{2... | collective-permute-start | bytes 393224 | tf_op jit(solution)/shard_map/ppermute | solution.py:23
  84.8 3.5 %collective-permute-start.11 = (f32[2,32,1024]{2,1,0:T(8,128)S(1)}, f32[2,32,1024]{2,1,0:T(8,128)S(1)}, u32[]{:S(2)}, u32[]{:S(2)}) collective-permute-start(f32[2,32,1024]{2,1,0:T(8,128)S(1)} %bitcast.91), channel_id=1, source_target_pairs={{0,8},{4,12},{8,16},{12,20},{16,24},{20,28},{1,9},{5,13},{9,17},{1... | collective-permute-start | bytes 786440 | tf_op jit(solution)/shard_map/ppermute | solution.py:23
  88.3 12.0 %collective-permute-done.8 = f32[4,32,1024]{2,1,0:T(8,128)S(1)} collective-permute-done((f32[4,32,1024]{2,1,0:T(8,128)S(1)}, f32[4,32,1024]{2,1,0:T(8,128)S(1)}, u32[]{:S(2)}, u32[]{:S(2)}) %collective-permute-start.8) | collective-permute-done | bytes 524320 | tf_op jit(solution)/shard_map/ppermute | solution.py:23
  100.3 3.1 %collective-permute-done.9 = f32[4,32,1024]{2,1,0:T(8,128)S(1)} collective-permute-done((f32[4,32,1024]{2,1,0:T(8,128)S(1)}, f32[4,32,1024]{2,1,0:T(8,128)S(1)}, u32[]{:S(2)}, u32[]{:S(2)}) %collective-permute-start.9) | collective-permute-done | bytes 524320 | tf_op jit(solution)/shard_map/ppermute | solution.py:23
  110.2 4.8 %collective-permute-start.13 = (f32[4,32,1024]{2,1,0:T(8,128)S(1)}, f32[4,32,1024]{2,1,0:T(8,128)S(1)}, u32[]{:S(2)}, u32[]{:S(2)}) collective-permute-start(f32[4,32,1024]{2,1,0:T(8,128)S(1)} %bitcast.82), channel_id=1, source_target_pairs={{0,4},{4,8},{8,12},{12,16},{16,20},{20,24},{24,28},{1,5},{5,9},{9,... | collective-permute-start | bytes 1572872 | tf_op jit(solution)/shard_map/ppermute | solution.py:23
  117.0 3.9 %collective-permute-start.16 = (f32[1,32,1024]{2,1,0:T(8,128)S(1)}, f32[1,32,1024]{2,1,0:T(8,128)S(1)}, u32[]{:S(2)}, u32[]{:S(2)}) collective-permute-start(f32[1,32,1024]{2,1,0:T(8,128)S(1)} %get-tuple-element.131), channel_id=1, source_target_pairs={{4,0},{8,4},{12,8},{16,12},{20,16},{24,20},{28,24},{5,1},{9,5},{13... | collective-permute-start | bytes 393224 | tf_op jit(solution)/shard_map/ppermute | solution.py:15
  121.0 20.8 %collective-permute-done.17 = f32[1,32,1024]{2,1,0:T(8,128)S(1)} collective-permute-done((f32[1,32,1024]{2,1,0:T(8,128)S(1)}, f32[1,32,1024]{2,1,0:T(8,128)S(1)}, u32[]{:S(2)}, u32[]{:S(2)}) %collective-permute-start.17) | collective-permute-done | bytes 131104 | tf_op jit(solution)/shard_map/ppermute | solution.py:14
  141.9 2.4 %collective-permute-start.14 = (f32[1,32,1024]{2,1,0:T(8,128)S(1)}, f32[1,32,1024]{2,1,0:T(8,128)S(1)}, u32[]{:S(2)}, u32[]{:S(2)}) collective-permute-start(f32[1,32,1024]{2,1,0:T(8,128)S(1)} %slice_bitcast_fusion), channel_id=1, source_target_pairs={{8,0},{12,4},{16,8},{20,12},{24,16},{28,20},{9,1},{13,5},{17,9},{2... | collective-permute-start | bytes 393224 | tf_op jit(solution)/shard_map/ppermute | solution.py:23
  144.2 3.5 %collective-permute-start.15 = (f32[2,32,1024]{2,1,0:T(8,128)S(1)}, f32[2,32,1024]{2,1,0:T(8,128)S(1)}, u32[]{:S(2)}, u32[]{:S(2)}) collective-permute-start(f32[2,32,1024]{2,1,0:T(8,128)S(1)} %bitcast.92), channel_id=1, source_target_pairs={{0,8},{4,12},{8,16},{12,20},{16,24},{20,28},{1,9},{5,13},{9,17},{1... | collective-permute-start | bytes 786440 | tf_op jit(solution)/shard_map/ppermute | solution.py:23
  149.2 4.9 %collective-permute-done.15 = f32[2,32,1024]{2,1,0:T(8,128)S(1)} collective-permute-done((f32[2,32,1024]{2,1,0:T(8,128)S(1)}, f32[2,32,1024]{2,1,0:T(8,128)S(1)}, u32[]{:S(2)}, u32[]{:S(2)}) %collective-permute-start.15) | collective-permute-done | bytes 262176 | tf_op jit(solution)/shard_map/ppermute | solution.py:23
  155.7 3.0 %collective-permute-start.19 = (f32[6,1,1024]{2,1,0:T(1,128)S(1)}, f32[6,1,1024]{2,1,0:T(1,128)S(1)}, u32[]{:S(2)}, u32[]{:S(2)}) collective-permute-start(f32[6,1,1024]{2,1,0:T(1,128)S(1)} %get-tuple-element.117), channel_id=1, source_target_pairs={{0,1},{1,2},{2,3},{4,5},{5,6},{6,7},{8,9},{9,10},{10,11},{12,13},{... | collective-permute-start | bytes 73736 | tf_op jit(solution)/shard_map/ppermute | solution.py:14
  (97 shorter events, 35.7 us)
Async XLA Ops:
  4.5 1.0 copy-start
  10.1 24.8 %collective-permute-start = (f32[4,32,1024]{2,1,0:T(8,128)S(1)}, f32[4,32,1024]{2,1,0:T(8,128)S(1)}, u32[]{:S(2)}, u32[]{:S(2)}) collective-permute-start(f32[4,32,1024]{2,1,0:T(8,128)S(1)} %bitcast.88), channel_id=1, source_target_pairs={{4,0},{8,4},{12,8},{16,12},{20,16},{24,20},{28,24},{5,1},{9,5},{13... | collective-permute-start | bytes 1572872 | tf_op jit(solution)/shard_map/ppermute | solution.py:23
  12.5 25.3 %collective-permute-start.1 = (f32[4,32,1024]{2,1,0:T(8,128)S(1)}, f32[4,32,1024]{2,1,0:T(8,128)S(1)}, u32[]{:S(2)}, u32[]{:S(2)}) collective-permute-start(f32[4,32,1024]{2,1,0:T(8,128)S(1)} %bitcast.85), channel_id=1, source_target_pairs={{0,4},{4,8},{8,12},{12,16},{16,20},{20,24},{24,28},{1,5},{5,9},{9,... | collective-permute-start | bytes 1572872 | tf_op jit(solution)/shard_map/ppermute | solution.py:23
  16.9 21.0 %collective-permute-start.2 = (f32[1,32,1024]{2,1,0:T(8,128)S(1)}, f32[1,32,1024]{2,1,0:T(8,128)S(1)}, u32[]{:S(2)}, u32[]{:S(2)}) collective-permute-start(f32[1,32,1024]{2,1,0:T(8,128)S(1)} %slice_bitcast_fusion.3), channel_id=1, source_target_pairs={{8,0},{12,4},{16,8},{20,12},{24,16},{28,20},{9,1},{13,5},{17,9},{2... | collective-permute-start | bytes 393224 | tf_op jit(solution)/shard_map/ppermute | solution.py:23
  19.3 18.7 %collective-permute-start.3 = (f32[2,32,1024]{2,1,0:T(8,128)S(1)}, f32[2,32,1024]{2,1,0:T(8,128)S(1)}, u32[]{:S(2)}, u32[]{:S(2)}) collective-permute-start(f32[2,32,1024]{2,1,0:T(8,128)S(1)} %bitcast.93), channel_id=1, source_target_pairs={{0,8},{4,12},{8,16},{12,20},{16,24},{20,28},{1,9},{5,13},{9,17},{1... | collective-permute-start | bytes 786440 | tf_op jit(solution)/shard_map/ppermute | solution.py:23
  42.7 24.8 %collective-permute-start.4 = (f32[4,32,1024]{2,1,0:T(8,128)S(1)}, f32[4,32,1024]{2,1,0:T(8,128)S(1)}, u32[]{:S(2)}, u32[]{:S(2)}) collective-permute-start(f32[4,32,1024]{2,1,0:T(8,128)S(1)} %bitcast.89), channel_id=1, source_target_pairs={{4,0},{8,4},{12,8},{16,12},{20,16},{24,20},{28,24},{5,1},{9,5},{13... | collective-permute-start | bytes 1572872 | tf_op jit(solution)/shard_map/ppermute | solution.py:23
  44.6 25.9 %collective-permute-start.5 = (f32[4,32,1024]{2,1,0:T(8,128)S(1)}, f32[4,32,1024]{2,1,0:T(8,128)S(1)}, u32[]{:S(2)}, u32[]{:S(2)}) collective-permute-start(f32[4,32,1024]{2,1,0:T(8,128)S(1)} %bitcast.86), channel_id=1, source_target_pairs={{0,4},{4,8},{8,12},{12,16},{16,20},{20,24},{24,28},{1,5},{5,9},{9,... | collective-permute-start | bytes 1572872 | tf_op jit(solution)/shard_map/ppermute | solution.py:23
  49.6 21.0 %collective-permute-start.6 = (f32[1,32,1024]{2,1,0:T(8,128)S(1)}, f32[1,32,1024]{2,1,0:T(8,128)S(1)}, u32[]{:S(2)}, u32[]{:S(2)}) collective-permute-start(f32[1,32,1024]{2,1,0:T(8,128)S(1)} %slice_bitcast_fusion.2), channel_id=1, source_target_pairs={{8,0},{12,4},{16,8},{20,12},{24,16},{28,20},{9,1},{13,5},{17,9},{2... | collective-permute-start | bytes 393224 | tf_op jit(solution)/shard_map/ppermute | solution.py:23
  52.0 18.7 %collective-permute-start.7 = (f32[2,32,1024]{2,1,0:T(8,128)S(1)}, f32[2,32,1024]{2,1,0:T(8,128)S(1)}, u32[]{:S(2)}, u32[]{:S(2)}) collective-permute-start(f32[2,32,1024]{2,1,0:T(8,128)S(1)} %bitcast.90), channel_id=1, source_target_pairs={{0,8},{4,12},{8,16},{12,20},{16,24},{20,28},{1,9},{5,13},{9,17},{1... | collective-permute-start | bytes 786440 | tf_op jit(solution)/shard_map/ppermute | solution.py:23
  75.5 24.8 %collective-permute-start.8 = (f32[4,32,1024]{2,1,0:T(8,128)S(1)}, f32[4,32,1024]{2,1,0:T(8,128)S(1)}, u32[]{:S(2)}, u32[]{:S(2)}) collective-permute-start(f32[4,32,1024]{2,1,0:T(8,128)S(1)} %bitcast.87), channel_id=1, source_target_pairs={{4,0},{8,4},{12,8},{16,12},{20,16},{24,20},{28,24},{5,1},{9,5},{13... | collective-permute-start | bytes 1572872 | tf_op jit(solution)/shard_map/ppermute | solution.py:23
  77.4 25.9 %collective-permute-start.9 = (f32[4,32,1024]{2,1,0:T(8,128)S(1)}, f32[4,32,1024]{2,1,0:T(8,128)S(1)}, u32[]{:S(2)}, u32[]{:S(2)}) collective-permute-start(f32[4,32,1024]{2,1,0:T(8,128)S(1)} %bitcast.84), channel_id=1, source_target_pairs={{0,4},{4,8},{8,12},{12,16},{16,20},{20,24},{24,28},{1,5},{5,9},{9,... | collective-permute-start | bytes 1572872 | tf_op jit(solution)/shard_map/ppermute | solution.py:23
  82.4 21.0 %collective-permute-start.10 = (f32[1,32,1024]{2,1,0:T(8,128)S(1)}, f32[1,32,1024]{2,1,0:T(8,128)S(1)}, u32[]{:S(2)}, u32[]{:S(2)}) collective-permute-start(f32[1,32,1024]{2,1,0:T(8,128)S(1)} %slice_bitcast_fusion.1), channel_id=1, source_target_pairs={{8,0},{12,4},{16,8},{20,12},{24,16},{28,20},{9,1},{13,5},{17,9},{2... | collective-permute-start | bytes 393224 | tf_op jit(solution)/shard_map/ppermute | solution.py:23
  84.8 18.7 %collective-permute-start.11 = (f32[2,32,1024]{2,1,0:T(8,128)S(1)}, f32[2,32,1024]{2,1,0:T(8,128)S(1)}, u32[]{:S(2)}, u32[]{:S(2)}) collective-permute-start(f32[2,32,1024]{2,1,0:T(8,128)S(1)} %bitcast.91), channel_id=1, source_target_pairs={{0,8},{4,12},{8,16},{12,20},{16,24},{20,28},{1,9},{5,13},{9,17},{1... | collective-permute-start | bytes 786440 | tf_op jit(solution)/shard_map/ppermute | solution.py:23
  108.1 6.9 %copy-start.1 = (f32[4,32,1024]{2,1,0:T(8,128)S(1)}, f32[4,32,1024]{2,1,0:T(8,128)}, u32[]{:S(2)}) copy-start(f32[4,32,1024]{2,1,0:T(8,128)} %param.23) | copy-start | bytes 1572868
  108.3 39.4 %collective-permute-start.12 = (f32[4,32,1024]{2,1,0:T(8,128)S(1)}, f32[4,32,1024]{2,1,0:T(8,128)S(1)}, u32[]{:S(2)}, u32[]{:S(2)}) collective-permute-start(f32[4,32,1024]{2,1,0:T(8,128)S(1)} %bitcast.83), channel_id=1, source_target_pairs={{4,0},{8,4},{12,8},{16,12},{20,16},{24,20},{28,24},{5,1},{9,5},{13... | collective-permute-start | bytes 1572872 | tf_op jit(solution)/shard_map/ppermute | solution.py:23
  110.2 37.5 %collective-permute-start.13 = (f32[4,32,1024]{2,1,0:T(8,128)S(1)}, f32[4,32,1024]{2,1,0:T(8,128)S(1)}, u32[]{:S(2)}, u32[]{:S(2)}) collective-permute-start(f32[4,32,1024]{2,1,0:T(8,128)S(1)} %bitcast.82), channel_id=1, source_target_pairs={{0,4},{4,8},{8,12},{12,16},{16,20},{20,24},{24,28},{1,5},{5,9},{9,... | collective-permute-start | bytes 1572872 | tf_op jit(solution)/shard_map/ppermute | solution.py:23
  115.1 26.7 %collective-permute-start.17 = (f32[1,32,1024]{2,1,0:T(8,128)S(1)}, f32[1,32,1024]{2,1,0:T(8,128)S(1)}, u32[]{:S(2)}, u32[]{:S(2)}) collective-permute-start(f32[1,32,1024]{2,1,0:T(8,128)S(1)} %get-tuple-element.132), channel_id=1, source_target_pairs={{0,4},{4,8},{8,12},{12,16},{16,20},{20,24},{24,28},{1,5},{5,9},{9,... | collective-permute-start | bytes 393224 | tf_op jit(solution)/shard_map/ppermute | solution.py:14
  117.0 37.1 %collective-permute-start.16 = (f32[1,32,1024]{2,1,0:T(8,128)S(1)}, f32[1,32,1024]{2,1,0:T(8,128)S(1)}, u32[]{:S(2)}, u32[]{:S(2)}) collective-permute-start(f32[1,32,1024]{2,1,0:T(8,128)S(1)} %get-tuple-element.131), channel_id=1, source_target_pairs={{4,0},{8,4},{12,8},{16,12},{20,16},{24,20},{28,24},{5,1},{9,5},{13... | collective-permute-start | bytes 393224 | tf_op jit(solution)/shard_map/ppermute | solution.py:15
  141.9 7.3 %collective-permute-start.14 = (f32[1,32,1024]{2,1,0:T(8,128)S(1)}, f32[1,32,1024]{2,1,0:T(8,128)S(1)}, u32[]{:S(2)}, u32[]{:S(2)}) collective-permute-start(f32[1,32,1024]{2,1,0:T(8,128)S(1)} %slice_bitcast_fusion), channel_id=1, source_target_pairs={{8,0},{12,4},{16,8},{20,12},{24,16},{28,20},{9,1},{13,5},{17,9},{2... | collective-permute-start | bytes 393224 | tf_op jit(solution)/shard_map/ppermute | solution.py:23
  144.2 9.8 %collective-permute-start.15 = (f32[2,32,1024]{2,1,0:T(8,128)S(1)}, f32[2,32,1024]{2,1,0:T(8,128)S(1)}, u32[]{:S(2)}, u32[]{:S(2)}) collective-permute-start(f32[2,32,1024]{2,1,0:T(8,128)S(1)} %bitcast.92), channel_id=1, source_target_pairs={{0,8},{4,12},{8,16},{12,20},{16,24},{20,28},{1,9},{5,13},{9,17},{1... | collective-permute-start | bytes 786440 | tf_op jit(solution)/shard_map/ppermute | solution.py:23
  154.3 6.9 %copy-start.2 = (bf16[4,32,1024]{2,1,0:T(8,128)(2,1)}, bf16[4,32,1024]{2,1,0:T(8,128)(2,1)S(1)}, u32[]{:S(2)}) copy-start(bf16[4,32,1024]{2,1,0:T(8,128)(2,1)S(1)} %get-tuple-element.99) | copy-start | bytes 786436
  154.4 4.3 %collective-permute-start.18 = (f32[6,1,1024]{2,1,0:T(1,128)S(1)}, f32[6,1,1024]{2,1,0:T(1,128)S(1)}, u32[]{:S(2)}, u32[]{:S(2)}) collective-permute-start(f32[6,1,1024]{2,1,0:T(1,128)S(1)} %get-tuple-element.116), channel_id=1, source_target_pairs={{1,0},{2,1},{3,2},{5,4},{6,5},{7,6},{9,8},{10,9},{11,10},{13,12},{... | collective-permute-start | bytes 73736 | tf_op jit(solution)/shard_map/ppermute | solution.py:15
  155.7 3.9 %collective-permute-start.19 = (f32[6,1,1024]{2,1,0:T(1,128)S(1)}, f32[6,1,1024]{2,1,0:T(1,128)S(1)}, u32[]{:S(2)}, u32[]{:S(2)}) collective-permute-start(f32[6,1,1024]{2,1,0:T(1,128)S(1)} %get-tuple-element.117), channel_id=1, source_target_pairs={{0,1},{1,2},{2,3},{4,5},{5,6},{6,7},{8,9},{9,10},{10,11},{12,13},{... | collective-permute-start | bytes 73736 | tf_op jit(solution)/shard_map/ppermute | solution.py:14
where the time goes:
time: 164 us; the launch traced here: 161 us
  waiting for transfers between devices  72.7 us (44%)
  starting transfers between devices  60.7 us (37%)
  matrix products  17.8 us (11%)
  local copies, waits for them, and re-layouts  4.67 us (3%)
  other arithmetic  3.98 us (2%)
    ppermute x16, waiting for transfers between devices, from_behind(): return lax.ppermute(array, axis, pairs)  51.1 us
    ppermute x16, starting transfers between devices, from_behind(): return lax.ppermute(array, axis, pairs)  50.5 us
    ppermute x2, waiting for transfers between devices, extended_2(): before = lax.ppermute(last, axis, up)  21.7 us
    dot_general x16, matrix products, shards(): jnp.dot(onehot, weights[offset] * values, precision=lax.Precision.HIGHEST...  17.8 us
    ppermute x2, starting transfers between devices, extended_2(): after = lax.ppermute(leading, axis, down)  5.21 us
    ppermute x2, starting transfers between devices, extended_2(): before = lax.ppermute(last, axis, up)  4.95 us
  transfers between devices with their start and end apart: 20, of which 10 were waited for; matrix products, arithmetic and copies ran while one was open for 1% of the time, Pallas kernels for 0%

commit v1 on v0

v1 whole, which is shorter than its diff:
```python
import functools

import jax
import jax.numpy as jnp
from jax import lax
from jax.experimental import pallas as pl
from jax.experimental.pallas import tpu as pltpu
from jax.sharding import PartitionSpec as P

BELOW = 5
ABOVE = 6
TILE = 8
MESH = pl.DeviceIdType.MESH


def kernel(
    slabs,
    pencils,
    land_ref,
    adj_ref,
    frac_ref,
    img_ref,
    adj_out,
    grad_out,
    land_buf,
    stage,
    cur,
    frac_buf,
    acc,
    tx_up,
    tx_dn,
    rx_lo,
    rx_hi,
    back_tx,
    back_rx,
    img_pad,
    land_sem,
    cur_sem,
    fl_sem,
    fr_sem,
    up_sem,
    dn_sem,
    back_sem,
    img_sem,
    halo_sem,
):
    s = lax.axis_index("slab")
    p = lax.axis_index("pencil")
    y = lax.rem(s, 2)
    other = 1 - y
    partner = s + 1 - 2 * y
    pair = lax.div(s, 2)
    has_lower = s >= 2
    has_upper = s + 2 < slabs

    rows, cols, line = adj_out.shape
    half = line // 2
    chunks = cols // TILE
    steps = frac_ref.shape[0]
    total = steps * chunks
    tall = 2 * rows
    span = BELOW + tall + ABOVE

    def remote(src, dst, sems, index, where):
        return pltpu.make_async_remote_copy(
            src_ref=src,
            dst_ref=dst,
            send_sem=sems.at[(0,) + index],
            recv_sem=sems.at[(1,) + index],
            device_id=where,
            device_id_type=MESH,
        )

    def frac_block(t, lanes):
        step = steps - 1 - lax.div(t, chunks)
        first = pl.multiple_of(lax.rem(t, chunks) * TILE, TILE)
        return frac_ref.at[step, :, pl.ds(first, TILE), pl.ds(pl.multiple_of(lanes * half, half), half)]

    def frac_local(t):
        return pltpu.make_async_copy(frac_block(t, y), frac_buf.at[t, y], fl_sem.at[t])

    def frac_remote(t, slot):
        return remote(frac_block(t, other), frac_buf.at[t, slot], fr_sem, (t,), {"slab": partner})

    def cur_remote(c, slot):
        return remote(stage.at[other, c], cur.at[c, slot], cur_sem, (c,), {"slab": partner})

    def land_remote(slot):
        return remote(land_ref, land_buf.at[slot], land_sem, (), {"slab": partner})

    def up_copy(t):
        return remote(tx_up.at[t], rx_lo.at[t], up_sem, (t,), {"slab": s + 2})

    def dn_copy(t):
        return remote(tx_dn.at[t], rx_hi.at[t], dn_sem, (t,), {"slab": s - 2})

    def back_copy(c):
        return remote(back_tx.at[c], back_rx.at[c], back_sem, (c,), {"slab": partner})

    center_cols = pl.ds(TILE, cols)
    image_copy = pltpu.make_async_copy(
        img_ref, img_pad.at[pl.ds(1, rows), center_cols], img_sem
    )
    halos = (
        (s + 1 < slabs, s >= 1, remote(
            img_ref.at[pl.ds(rows - 1, 1)], img_pad.at[pl.ds(0, 1), center_cols],
            halo_sem, (0,), {"slab": s + 1})),
        (s >= 1, s + 1 < slabs, remote(
            img_ref.at[pl.ds(0, 1)], img_pad.at[pl.ds(rows + 1, 1), center_cols],
            halo_sem, (1,), {"slab": s - 1})),
        (p + 1 < pencils, p >= 1, remote(
            img_ref.at[:, pl.ds(cols - TILE, TILE)], img_pad.at[pl.ds(1, rows), pl.ds(0, TILE)],
            halo_sem, (2,), {"pencil": p + 1})),
        (p >= 1, p + 1 < pencils, remote(
            img_ref.at[:, pl.ds(0, TILE)], img_pad.at[pl.ds(1, rows), pl.ds(cols + TILE, TILE)],
            halo_sem, (3,), {"pencil": p - 1})),
    )

    barrier = pltpu.get_barrier_semaphore()
    for there, where in (
        (s >= 1, {"slab": s - 1}),
        (s + 1 < slabs, {"slab": s + 1}),
        (has_lower, {"slab": s - 2}),
        (has_upper, {"slab": s + 2}),
        (p >= 1, {"pencil": p - 1}),
        (p + 1 < pencils, {"pencil": p + 1}),
    ):
        @pl.when(there)
        def _():
            pl.semaphore_signal(barrier, inc=1, device_id=where, device_id_type=MESH)

    lax.fori_loop(0, total, lambda t, z: (frac_local(t).start(), z)[1], 0)
    image_copy.start()
    land_buf[y] = land_ref[...]
    for q in range(cols // (2 * TILE)):
        for h in range(2):
            wide = adj_ref[:, 2 * TILE * q : 2 * TILE * (q + 1), half * h : half * (h + 1)]
            wide = wide.astype(jnp.float32)
            stage[h, 2 * q] = wide[:, :TILE]
            stage[h, 2 * q + 1] = wide[:, TILE:]

    peers = sum(
        jnp.where(there, 1, 0)
        for there in (s >= 1, s + 1 < slabs, has_lower, has_upper, p >= 1, p + 1 < pencils)
    )
    pl.semaphore_wait(barrier, peers)

    land_remote(y).start()

    def start_first(c, z):
        cur_remote(c, y).start()
        frac_remote(c, y).start()
        return z

    lax.fori_loop(0, chunks, start_first, 0)
    lax.fori_loop(chunks, total, lambda t, z: (frac_remote(t, y).start(), z)[1], 0)
    for send, _, copy in halos:
        @pl.when(send)
        def _():
            copy.start()

    for c in range(chunks):
        cur[c, y] = stage[y, c]
    land_remote(other).wait_recv()

    def splat(t, c, values):
        frac_local(t).wait()
        frac_remote(t, other).wait_recv()
        parts = []
        hots = []
        target = lax.broadcasted_iota(jnp.int32, (span * TILE, 4 * rows * TILE), 0)
        target = target + (pair * tall - BELOW) * TILE
        for h in range(2):
            f = frac_buf[t, h].reshape(rows * TILE, half)
            v = values[h].reshape(rows * TILE, half)
            rest = 1.0 - f
            square = f * f
            cube = square * f
            sixth = v * (1.0 / 6.0)
            parts.append(rest * rest * rest * sixth)
            parts.append((3.0 * cube - 6.0 * square + 4.0) * sixth)
            parts.append((-3.0 * cube + 3.0 * square + 3.0 * f + 1.0) * sixth)
            parts.append(cube * sixth)
            land = land_buf[h, pl.ds(t, 1), :]
            hots.append(jnp.where(target == land, 1.0, 0.0).astype(jnp.bfloat16))
        hot = jnp.concatenate(hots, axis=1)
        high = [part.astype(jnp.bfloat16) for part in parts]
        low = [(a - b.astype(jnp.float32)).astype(jnp.bfloat16) for a, b in zip(parts, high)]
        out = jnp.dot(hot, jnp.concatenate(high, axis=0), preferred_element_type=jnp.float32)
        out = out + jnp.dot(hot, jnp.concatenate(low, axis=0), preferred_element_type=jnp.float32)
        out = out.reshape(span, TILE, half)
        tx_dn[t] = out[:BELOW]
        tx_up[t] = out[BELOW + tall :]

        @pl.when(has_upper)
        def _():
            up_copy(t).start()

        @pl.when(has_lower)
        def _():
            dn_copy(t).start()

        acc[c] = out[BELOW : BELOW + tall]

    def combine(t, c):
        @pl.when(has_lower)
        def _():
            up_copy(t).wait_recv()
            acc[c, :ABOVE] += rx_lo[t]

        @pl.when(has_upper)
        def _():
            dn_copy(t).wait_recv()
            acc[c, tall - BELOW :] += rx_hi[t]

        whole = acc[c].astype(jnp.bfloat16).astype(jnp.float32)
        return whole.reshape(2, rows, TILE, half)

    def first_step(c, z):
        cur_remote(c, other).wait_recv()
        splat(c, c, cur[c])
        return z

    lax.fori_loop(0, chunks, first_step, 0)

    def later_step(t, z):
        c = lax.rem(t, chunks)
        splat(t, c, combine(t - chunks, c))
        return z

    lax.fori_loop(chunks, total, later_step, 0)

    image_copy.wait()
    for index, (_, receive, copy) in enumerate(halos):
        @pl.when(receive)
        def _():
            copy.wait_recv()

        @pl.when(jnp.logical_not(receive))
        def _():
            if index < 2:
                edge = 0 if index == 0 else rows + 1
                img_pad[edge, TILE : TILE + cols] = jnp.zeros((cols, line), jnp.float32)
            else:
                edge = 0 if index == 2 else cols + TILE
                img_pad[1 : rows + 1, edge : edge + TILE] = jnp.zeros((rows, TILE, line), jnp.float32)

    lane = lax.broadcasted_iota(jnp.int32, (cols, line), 1)

    def gradient(r, z):
        grad_out[0, r] = (img_pad[r + 2, TILE : TILE + cols] - img_pad[r, TILE : TILE + cols]) * 0.5
        grad_out[1, r] = (
            img_pad[r + 1, TILE + 1 : TILE + cols + 1] - img_pad[r + 1, TILE - 1 : TILE + cols - 1]
        ) * 0.5
        center = img_pad[r + 1, TILE : TILE + cols]
        after = jnp.where(lane == line - 1, 0.0, pltpu.roll(center, line - 1, 1))
        before = jnp.where(lane == 0, 0.0, pltpu.roll(center, 1, 1))
        grad_out[2, r] = (after - before) * 0.5
        return z

    lax.fori_loop(0, rows, gradient, 0)

    def finish(c, z):
        combine_out = combine(total - chunks + c, c)
        acc[c] = combine_out.reshape(tall, TILE, half)
        back_tx[c] = acc[c, pl.ds(other * rows, rows)]
        back_copy(c).start()
        first = pl.multiple_of(c * TILE, TILE)
        adj_out[:, pl.ds(first, TILE), pl.ds(pl.multiple_of(y * half, half), half)] = acc[c, pl.ds(y * rows, rows)]
        return z

    lax.fori_loop(0, chunks, finish, 0)

    def collect(c, z):
        back_copy(c).wait_recv()
        first = pl.multiple_of(c * TILE, TILE)
        adj_out[:, pl.ds(first, TILE), pl.ds(pl.multiple_of(other * half, half), half)] = back_rx[c]
        return z

    lax.fori_loop(0, chunks, collect, 0)

    land_remote(y).wait_send()
    lax.fori_loop(0, chunks, lambda c, z: (cur_remote(c, y).wait_send(), back_copy(c).wait_send(), z)[2], 0)

    def drain(t, z):
        frac_remote(t, y).wait_send()

        @pl.when(has_upper)
        def _():
            up_copy(t).wait_send()

        @pl.when(has_lower)
        def _():
            dn_copy(t).wait_send()

        return z

    lax.fori_loop(0, total, drain, 0)
    for send, _, copy in halos:
        @pl.when(send)
        def _():
            copy.wait_send()


def shards(slabs, pencils, final_adjoint, departure, fraction, image):
    steps, rows, cols = departure.shape
    line = image.shape[2]
    half = line // 2
    chunks = cols // TILE
    total = steps * chunks
    tall = 2 * rows
    assert slabs % 2 == 0 and ABOVE <= tall and cols % (2 * TILE) == 0 and half % 128 == 0

    land = departure[::-1].reshape(steps, rows, chunks, TILE).transpose(0, 2, 1, 3)
    land = land[:, :, None] + (jnp.arange(4, dtype=jnp.int32) - 1)[:, None, None]
    land = (land * TILE + jnp.arange(TILE, dtype=jnp.int32)).reshape(total, 4 * rows * TILE)

    f32 = jnp.float32
    dma = pltpu.SemaphoreType.DMA
    vmem = pl.BlockSpec(memory_space=pltpu.VMEM)
    hbm = pl.BlockSpec(memory_space=pl.ANY)
    adjoint, gradient = pl.pallas_call(
        functools.partial(kernel, slabs, pencils),
        name="splat",
        out_shape=(
            jax.ShapeDtypeStruct((rows, cols, line), f32),
            jax.ShapeDtypeStruct((3, rows, cols, line), f32),
        ),
        in_specs=[vmem, vmem, hbm, hbm],
        out_specs=(vmem, vmem),
        scratch_shapes=[
            pltpu.VMEM((2, total, 4 * rows * TILE), jnp.int32),
            pltpu.VMEM((2, chunks, rows, TILE, half), f32),
            pltpu.VMEM((chunks, 2, rows, TILE, half), f32),
            pltpu.VMEM((total, 2, rows, TILE, half), f32),
            pltpu.VMEM((chunks, tall, TILE, half), f32),
            pltpu.VMEM((total, ABOVE, TILE, half), f32),
            pltpu.VMEM((total, BELOW, TILE, half), f32),
            pltpu.VMEM((total, ABOVE, TILE, half), f32),
            pltpu.VMEM((total, BELOW, TILE, half), f32),
            pltpu.VMEM((chunks, rows, TILE, half), f32),
            pltpu.VMEM((chunks, rows, TILE, half), f32),
            pltpu.VMEM((rows + 2, cols + 2 * TILE, line), f32),
            dma((2,)),
            dma((2, chunks)),
            dma((total,)),
            dma((2, total)),
            dma((2, total)),
            dma((2, total)),
            dma((2, chunks)),
            dma(()),
            dma((2, 4)),
        ],
        compiler_params=pltpu.CompilerParams(
            collective_id=0, has_side_effects=True, vmem_limit_bytes=40 * 1024 * 1024
        ),
    )(land, final_adjoint, fraction, image)
    return adjoint.astype(jnp.bfloat16), adjoint[None] * gradient


def solution(mesh):
    in_specs = (
        P("slab", "pencil", None),
        P(None, "slab", "pencil"),
        P(None, "slab", "pencil", None),
        P("slab", "pencil", None),
    )
    out_specs = (P("slab", "pencil", None), P(None, "slab", "pencil", None))
    body = functools.partial(shards, mesh.shape["slab"], mesh.shape["pencil"])
    return jax.shard_map(body, mesh=mesh, in_specs=in_specs, out_specs=out_specs, check_vma=False)
```

time: 164 us -> 59.2 us (0.36); the launches traced: 161 us -> 59 us
  waiting for transfers between devices: 72.7 us -> 0 us
  starting transfers between devices: 60.7 us -> 0 us
  Pallas kernels: 0 us -> 51.4 us
  matrix products: 17.8 us -> 0 us
  other arithmetic: 3.98 us -> 2.04 us
    ppermute x20 -> x0, waiting for transfers between devices: 72.7 us -> none  [the longest x16 51.1 us: from_behind(): return lax.ppermute(array, axis, pairs)]
    ppermute x20 -> x0, starting transfers between devices: 60.7 us -> none  [the longest x16 50.5 us: from_behind(): return lax.ppermute(array, axis, pairs)]
    pallas_call x0 -> x1, Pallas kernels: none -> 51.4 us  [shards(): pl.pallas_call(functools.partial(kernel, slabs, pencils), name='splat', o...]
    dot_general x16 -> x0, matrix products: 17.8 us -> none  [shards(): jnp.dot(onehot, weights[offset] * values, precision=lax.Precision.HIGHEST...]
    unnamed x7 -> x6, local copies, waits for them, and re-layouts: 0.76 us -> 3.58 us
    slice x15 -> x0, local copies, waits for them, and re-layouts: 2.49 us -> none  [the longest x1 1.67 us: shards(): weights = spline_weights(fraction[step].reshape(blocks, line))]
    another operation x3 -> x0, other arithmetic: 1.79 us -> none  [shards(): jnp.stack([weight_field * along_first, weight_field * along_second, weigh...]
  transfers between devices with their start and end apart: 20 -> 0, of which waited for: 10 -> 0; matrix products, arithmetic and copies ran while one was open for 1% -> 0% of each run, Pallas kernels for 0% -> 0%
where the time goes in v1:
time: 59.2 us; the launch traced here: 59 us
  Pallas kernels  51.4 us (87%)
  local copies, waits for them, and re-layouts  4.81 us (8%)
  other arithmetic  2.04 us (3%)
  between operations  0.68 us (1%)
    pallas_call x1, Pallas kernels, shards(): pl.pallas_call(functools.partial(kernel, slabs, pencils), name='splat', o...  51.4 us
    unnamed x6, local copies, waits for them, and re-layouts  3.58 us
    mul x1, other arithmetic, shards(): return (adjoint.astype(jnp.bfloat16), adjoint[None] * gradient)  1.29 us

profile of v1, /device:TPU:20, one launch (start us, length us, event | category | flops | bytes accessed | tf_op | source)
XLA Modules:
  0.0 59.0 jit_solution(15432615783329747660)
XLA Ops:
  0.6 0.1 add.40
  0.7 0.1 add.41
  0.8 0.7 %rev.3 = s32[4,4,32]{2,1,0:T(4,128)S(1)} reverse(s32[4,4,32]{2,1,0:T(4,128)} %param.5), dimensions={0} | reverse | bytes 4096 | tf_op jit(solution)/shard_map/rev | solution.py:314
  1.5 0.1 add.45
  1.6 0.1 reshape.17
  1.7 0.2 add.39
  1.9 0.0 copy-start
  1.9 1.6 %copy-done = f32[4,4,32,1024]{3,2,1,0:T(8,128)S(1)} copy-done((f32[4,4,32,1024]{3,2,1,0:T(8,128)S(1)}, f32[4,4,32,1024]{3,2,1,0:T(8,128)}, u32[]{:S(2)}) %copy-start) | copy-done | bytes 2097176
  3.5 0.0 copy-start.1
  3.5 1.0 %copy-done.1 = f32[4,32,1024]{2,1,0:T(8,128)S(1)} copy-done((f32[4,32,1024]{2,1,0:T(8,128)S(1)}, f32[4,32,1024]{2,1,0:T(8,128)}, u32[]{:S(2)}) %copy-start.1) | copy-done | bytes 524312
  4.5 0.0 copy-start.2
  4.6 0.9 %copy-done.2 = bf16[4,32,1024]{2,1,0:T(8,128)(2,1)S(1)} copy-done((bf16[4,32,1024]{2,1,0:T(8,128)(2,1)S(1)}, bf16[4,32,1024]{2,1,0:T(8,128)(2,1)}, u32[]{:S(2)}) %copy-start.2) | copy-done | bytes 262168
  5.5 51.4 %splat.1 = (f32[4,32,1024]{2,1,0:T(8,128)S(1)}, f32[3,4,32,1024]{3,2,1,0:T(8,128)S(1)}) custom-call(s32[16,128]{1,0:T(8,128)S(1)} %multiply_add_fusion.land_ref, bf16[4,32,1024]{2,1,0:T(8,128)(2,1)S(1)} %copy-done.2, f32[4,4,32,1024]{3,2,1,0:T(8,128)S(1)} %copy-done, f32[4,32,1024]{2,1,0:T(8,128)S(1)} %copy-done.1), custom_call_target="tpu_custom_call" | custom-call | tf_op jit(solution)/shard_map/splat/pallas_call | solution.py:322
  56.9 1.3 %broadcast_multiply_fusion = f32[3,4,32,1024]{3,2,1,0:T(8,128)} fusion(f32[3,4,32,1024]{3,2,1,0:T(8,128)S(1)} %get-tuple-element.5, f32[4,32,1024]{2,1,0:T(8,128)S(1)} %get-tuple-element.4), kind=kLoop, calls=%fused_computation | loop fusion | flops 393216 | bytes 3670016 | tf_op jit(solution)/shard_map/mul | solution.py:358
  58.2 0.7 %convert_element_type.3 = bf16[4,32,1024]{2,1,0:T(8,128)(2,1)} convert(f32[4,32,1024]{2,1,0:T(8,128)S(1)} %get-tuple-element.4) | non-fusion elementwise | flops 131072 | bytes 786432 | tf_op jit(solution)/shard_map/convert_element_type | solution.py:358
  (5 shorter events, 0.0 us)
Async XLA Ops:
  1.9 1.6 %copy-start = (f32[4,4,32,1024]{3,2,1,0:T(8,128)S(1)}, f32[4,4,32,1024]{3,2,1,0:T(8,128)}, u32[]{:S(2)}) copy-start(f32[4,4,32,1024]{3,2,1,0:T(8,128)} %frac_ref.1) | copy-start | bytes 6291460
  3.5 1.0 %copy-start.1 = (f32[4,32,1024]{2,1,0:T(8,128)S(1)}, f32[4,32,1024]{2,1,0:T(8,128)}, u32[]{:S(2)}) copy-start(f32[4,32,1024]{2,1,0:T(8,128)} %img_ref.1) | copy-start | bytes 1572868
  4.5 0.9 %copy-start.2 = (bf16[4,32,1024]{2,1,0:T(8,128)(2,1)S(1)}, bf16[4,32,1024]{2,1,0:T(8,128)(2,1)}, u32[]{:S(2)}) copy-start(bf16[4,32,1024]{2,1,0:T(8,128)(2,1)} %adj_ref.1) | copy-start | bytes 786436

commit v2 on v1

--- a/solution.py
+++ b/solution.py
@@ -10,19 +10,22 @@
 BELOW = 5
 ABOVE = 6
 TILE = 8
+WIDTH = 256
 MESH = pl.DeviceIdType.MESH
 
 
 def kernel(
     slabs,
     pencils,
-    land_ref,
+    dep_ref,
     adj_ref,
     frac_ref,
     img_ref,
     adj_out,
     grad_out,
+    dep_buf,
     land_buf,
+    adj_buf,
     stage,
     cur,
     frac_buf,
@@ -34,7 +37,8 @@
     back_tx,
     back_rx,
     img_pad,
-    land_sem,
+    dep_sem,
+    adj_sem,
     cur_sem,
     fl_sem,
     fr_sem,
@@ -55,7 +59,10 @@
 
     rows, cols, line = adj_out.shape
     half = line // 2
-    chunks = cols // TILE
+    width = stage.shape[-1]
+    lanes_parts = half // width
+    tiles = cols // TILE
+    chunks = tiles * lanes_parts
     steps = frac_ref.shape[0]
     total = steps * chunks
     tall = 2 * rows
@@ -71,10 +78,14 @@
             device_id_type=MESH,
         )
 
-    def frac_block(t, lanes):
+    def place(c, side):
+        first = pl.multiple_of(lax.div(c, lanes_parts) * TILE, TILE)
+        lanes = pl.multiple_of(side * half + lax.rem(c, lanes_parts) * width, width)
+        return pl.ds(first, TILE), pl.ds(lanes, width)
+
+    def frac_block(t, side):
         step = steps - 1 - lax.div(t, chunks)
-        first = pl.multiple_of(lax.rem(t, chunks) * TILE, TILE)
-        return frac_ref.at[step, :, pl.ds(first, TILE), pl.ds(pl.multiple_of(lanes * half, half), half)]
+        return frac_ref.at[(step, slice(None)) + place(lax.rem(t, chunks), side)]
 
     def frac_local(t):
         return pltpu.make_async_copy(frac_block(t, y), frac_buf.at[t, y], fl_sem.at[t])
@@ -85,8 +96,8 @@
     def cur_remote(c, slot):
         return remote(stage.at[other, c], cur.at[c, slot], cur_sem, (c,), {"slab": partner})
 
-    def land_remote(slot):
-        return remote(land_ref, land_buf.at[slot], land_sem, (), {"slab": partner})
+    def dep_remote(slot):
+        return remote(dep_ref, dep_buf.at[slot], dep_sem, (), {"slab": partner})
 
     def up_copy(t):
         return remote(tx_up.at[t], rx_lo.at[t], up_sem, (t,), {"slab": s + 2})
@@ -129,15 +140,20 @@
         def _():
             pl.semaphore_signal(barrier, inc=1, device_id=where, device_id_type=MESH)
 
+    adj_copy = pltpu.make_async_copy(adj_ref, adj_buf, adj_sem)
+    adj_copy.start()
     lax.fori_loop(0, total, lambda t, z: (frac_local(t).start(), z)[1], 0)
     image_copy.start()
-    land_buf[y] = land_ref[...]
+    dep_buf[y] = dep_ref[...]
+    adj_copy.wait()
     for q in range(cols // (2 * TILE)):
         for h in range(2):
-            wide = adj_ref[:, 2 * TILE * q : 2 * TILE * (q + 1), half * h : half * (h + 1)]
-            wide = wide.astype(jnp.float32)
-            stage[h, 2 * q] = wide[:, :TILE]
-            stage[h, 2 * q + 1] = wide[:, TILE:]
+            for k in range(lanes_parts):
+                first = half * h + width * k
+                wide = adj_buf[:, 2 * TILE * q : 2 * TILE * (q + 1), first : first + width]
+                wide = wide.astype(jnp.float32)
+                stage[h, 2 * q * lanes_parts + k] = wide[:, :TILE]
+                stage[h, (2 * q + 1) * lanes_parts + k] = wide[:, TILE:]
 
     peers = sum(
         jnp.where(there, 1, 0)
@@ -145,11 +161,11 @@
     )
     pl.semaphore_wait(barrier, peers)
 
-    land_remote(y).start()
+    dep_remote(y).start()
 
     def start_first(c, z):
+        frac_remote(c, y).start()
         cur_remote(c, y).start()
-        frac_remote(c, y).start()
         return z
 
     lax.fori_loop(0, chunks, start_first, 0)
@@ -161,7 +177,36 @@
 
     for c in range(chunks):
         cur[c, y] = stage[y, c]
-    land_remote(other).wait_recv()
+
+    lane = lax.broadcasted_iota(jnp.int32, (steps, 4 * rows * TILE), 1)
+    lane_row = lax.rem(lax.div(lane, TILE), rows)
+    fixed = lane_row + lax.div(lane, rows * TILE) - 1 + BELOW
+    fixed = fixed * TILE + lax.rem(lane, TILE)
+    pick_lane = lax.broadcasted_iota(jnp.int32, (cols, 4 * rows * TILE), 1)
+    pick_col = lax.broadcasted_iota(jnp.int32, (cols, 4 * rows * TILE), 0)
+    keep_lane = lax.broadcasted_iota(jnp.int32, (steps * rows, 4 * rows * TILE), 1)
+    keep_row = lax.broadcasted_iota(jnp.int32, (steps * rows, 4 * rows * TILE), 0)
+    keep = lax.rem(keep_row, rows) == lax.rem(lax.div(keep_lane, TILE), rows)
+    group_step = lax.broadcasted_iota(jnp.int32, (steps, steps * rows), 0)
+    group_row = lax.broadcasted_iota(jnp.int32, (steps, steps * rows), 1)
+    group = jnp.where(group_step == lax.div(group_row, rows), 1.0, 0.0).astype(jnp.bfloat16)
+    row_of = lax.broadcasted_iota(jnp.int32, (rows, cols), 0)
+
+    def landing(h):
+        first_row = pair * tall + h * rows
+        moved = jnp.concatenate([dep_buf[h, k] - row_of - first_row for k in range(steps)], axis=0)
+        moved = moved.astype(jnp.float32).astype(jnp.bfloat16)
+        for tile in range(tiles):
+            pick = pick_col == tile * TILE + lax.rem(pick_lane, TILE)
+            pick = jnp.where(pick, 1.0, 0.0).astype(jnp.bfloat16)
+            spread = jnp.dot(moved, pick, preferred_element_type=jnp.float32)
+            spread = jnp.where(keep, spread, 0.0).astype(jnp.bfloat16)
+            by_step = jnp.dot(group, spread, preferred_element_type=jnp.float32)
+            land_buf[h, tile] = fixed + h * rows * TILE + by_step.astype(jnp.int32) * TILE
+
+    landing(y)
+    dep_remote(other).wait_recv()
+    landing(other)
 
     def splat(t, c, values):
         frac_local(t).wait()
@@ -169,10 +214,11 @@
         parts = []
         hots = []
         target = lax.broadcasted_iota(jnp.int32, (span * TILE, 4 * rows * TILE), 0)
-        target = target + (pair * tall - BELOW) * TILE
+        tile = lax.div(c, lanes_parts)
+        step = steps - 1 - lax.div(t, chunks)
         for h in range(2):
-            f = frac_buf[t, h].reshape(rows * TILE, half)
-            v = values[h].reshape(rows * TILE, half)
+            f = frac_buf[t, h].reshape(rows * TILE, width)
+            v = values[h].reshape(rows * TILE, width)
             rest = 1.0 - f
             square = f * f
             cube = square * f
@@ -181,14 +227,14 @@
             parts.append((3.0 * cube - 6.0 * square + 4.0) * sixth)
             parts.append((-3.0 * cube + 3.0 * square + 3.0 * f + 1.0) * sixth)
             parts.append(cube * sixth)
-            land = land_buf[h, pl.ds(t, 1), :]
+            land = land_buf[h, tile, pl.ds(step, 1), :]
             hots.append(jnp.where(target == land, 1.0, 0.0).astype(jnp.bfloat16))
         hot = jnp.concatenate(hots, axis=1)
         high = [part.astype(jnp.bfloat16) for part in parts]
         low = [(a - b.astype(jnp.float32)).astype(jnp.bfloat16) for a, b in zip(parts, high)]
         out = jnp.dot(hot, jnp.concatenate(high, axis=0), preferred_element_type=jnp.float32)
         out = out + jnp.dot(hot, jnp.concatenate(low, axis=0), preferred_element_type=jnp.float32)
-        out = out.reshape(span, TILE, half)
+        out = out.reshape(span, TILE, width)
         tx_dn[t] = out[:BELOW]
         tx_up[t] = out[BELOW + tall :]
 
@@ -214,7 +260,7 @@
             acc[c, tall - BELOW :] += rx_hi[t]
 
         whole = acc[c].astype(jnp.bfloat16).astype(jnp.float32)
-        return whole.reshape(2, rows, TILE, half)
+        return whole.reshape(2, rows, TILE, width)
 
     def first_step(c, z):
         cur_remote(c, other).wait_recv()
@@ -262,24 +308,22 @@
 
     def finish(c, z):
         combine_out = combine(total - chunks + c, c)
-        acc[c] = combine_out.reshape(tall, TILE, half)
+        acc[c] = combine_out.reshape(tall, TILE, width)
         back_tx[c] = acc[c, pl.ds(other * rows, rows)]
         back_copy(c).start()
-        first = pl.multiple_of(c * TILE, TILE)
-        adj_out[:, pl.ds(first, TILE), pl.ds(pl.multiple_of(y * half, half), half)] = acc[c, pl.ds(y * rows, rows)]
+        adj_out[(slice(None),) + place(c, y)] = acc[c, pl.ds(y * rows, rows)]
         return z
 
     lax.fori_loop(0, chunks, finish, 0)
 
     def collect(c, z):
         back_copy(c).wait_recv()
-        first = pl.multiple_of(c * TILE, TILE)
-        adj_out[:, pl.ds(first, TILE), pl.ds(pl.multiple_of(other * half, half), half)] = back_rx[c]
+        adj_out[(slice(None),) + place(c, other)] = back_rx[c]
         return z
 
     lax.fori_loop(0, chunks, collect, 0)
 
-    land_remote(y).wait_send()
+    dep_remote(y).wait_send()
     lax.fori_loop(0, chunks, lambda c, z: (cur_remote(c, y).wait_send(), back_copy(c).wait_send(), z)[2], 0)
 
     def drain(t, z):
@@ -306,19 +350,17 @@
     steps, rows, cols = departure.shape
     line = image.shape[2]
     half = line // 2
-    chunks = cols // TILE
+    width = WIDTH if half % WIDTH == 0 else half
+    tiles = cols // TILE
+    chunks = tiles * (half // width)
     total = steps * chunks
     tall = 2 * rows
     assert slabs % 2 == 0 and ABOVE <= tall and cols % (2 * TILE) == 0 and half % 128 == 0
 
-    land = departure[::-1].reshape(steps, rows, chunks, TILE).transpose(0, 2, 1, 3)
-    land = land[:, :, None] + (jnp.arange(4, dtype=jnp.int32) - 1)[:, None, None]
-    land = (land * TILE + jnp.arange(TILE, dtype=jnp.int32)).reshape(total, 4 * rows * TILE)
-
     f32 = jnp.float32
     dma = pltpu.SemaphoreType.DMA
     vmem = pl.BlockSpec(memory_space=pltpu.VMEM)
-    hbm = pl.BlockSpec(memory_space=pl.ANY)
+    hbm = pl.BlockSpec(memory_space=pltpu.HBM)
     adjoint, gradient = pl.pallas_call(
         functools.partial(kernel, slabs, pencils),
         name="splat",
@@ -326,22 +368,25 @@
             jax.ShapeDtypeStruct((rows, cols, line), f32),
             jax.ShapeDtypeStruct((3, rows, cols, line), f32),
         ),
-        in_specs=[vmem, vmem, hbm, hbm],
+        in_specs=[vmem, hbm, hbm, hbm],
         out_specs=(vmem, vmem),
         scratch_shapes=[
-            pltpu.VMEM((2, total, 4 * rows * TILE), jnp.int32),
-            pltpu.VMEM((2, chunks, rows, TILE, half), f32),
-            pltpu.VMEM((chunks, 2, rows, TILE, half), f32),
-            pltpu.VMEM((total, 2, rows, TILE, half), f32),
-            pltpu.VMEM((chunks, tall, TILE, half), f32),
-            pltpu.VMEM((total, ABOVE, TILE, half), f32),
-            pltpu.VMEM((total, BELOW, TILE, half), f32),
-            pltpu.VMEM((total, ABOVE, TILE, half), f32),
-            pltpu.VMEM((total, BELOW, TILE, half), f32),
-            pltpu.VMEM((chunks, rows, TILE, half), f32),
-            pltpu.VMEM((chunks, rows, TILE, half), f32),
+            pltpu.VMEM((2, steps, rows, cols), jnp.int32),
+            pltpu.VMEM((2, tiles, steps, 4 * rows * TILE), jnp.int32),
+            pltpu.VMEM((rows, cols, line), jnp.bfloat16),
+            pltpu.VMEM((2, chunks, rows, TILE, width), f32),
+            pltpu.VMEM((chunks, 2, rows, TILE, width), f32),
+            pltpu.VMEM((total, 2, rows, TILE, width), f32),
+            pltpu.VMEM((chunks, tall, TILE, width), f32),
+            pltpu.VMEM((total, ABOVE, TILE, width), f32),
+            pltpu.VMEM((total, BELOW, TILE, width), f32),
+            pltpu.VMEM((total, ABOVE, TILE, width), f32),
+            pltpu.VMEM((total, BELOW, TILE, width), f32),
+            pltpu.VMEM((chunks, rows, TILE, width), f32),
+            pltpu.VMEM((chunks, rows, TILE, width), f32),
             pltpu.VMEM((rows + 2, cols + 2 * TILE, line), f32),
             dma((2,)),
+            dma(()),
             dma((2, chunks)),
             dma((total,)),
             dma((2, total)),
@@ -354,7 +399,7 @@
         compiler_params=pltpu.CompilerParams(
             collective_id=0, has_side_effects=True, vmem_limit_bytes=40 * 1024 * 1024
         ),
-    )(land, final_adjoint, fraction, image)
+    )(departure, final_adjoint, fraction, image)
     return adjoint.astype(jnp.bfloat16), adjoint[None] * gradient
 
 

time: 59.2 us -> 58.6 us (0.990)
    rev x1 -> x0, local copies, waits for them, and re-layouts: 0.7 us -> none  [shards(): departure[::-1].reshape(steps, rows, chunks, TILE).transpose(0, 2, 1, 3)]
    unnamed x6 -> x8, local copies, waits for them, and re-layouts: 3.58 us -> 4.27 us
where the time goes in v2:
time: 58.6 us; the launch traced here: 58.4 us
  Pallas kernels  51.4 us (88%)
  local copies, waits for them, and re-layouts  4.27 us (7%)
  other arithmetic  2.03 us (3%)
  between operations  0.65 us (1%)
    pallas_call x1, Pallas kernels, shards(): pl.pallas_call(functools.partial(kernel, slabs, pencils), name='splat', o...  51.4 us
    unnamed x8, local copies, waits for them, and re-layouts  4.27 us
    mul x1, other arithmetic, shards(): return (adjoint.astype(jnp.bfloat16), adjoint[None] * gradient)  1.29 us

profile of v2, /device:TPU:20, one launch (start us, length us, event | category | flops | bytes accessed | tf_op | source)
XLA Modules:
  0.0 58.4 jit_solution(10781574808959265180)
XLA Ops:
  0.6 0.0 copy-start
  0.6 1.6 %copy-done = f32[4,4,32,1024]{3,2,1,0:T(8,128)S(1)} copy-done((f32[4,4,32,1024]{3,2,1,0:T(8,128)S(1)}, f32[4,4,32,1024]{3,2,1,0:T(8,128)}, u32[]{:S(2)}) %copy-start) | copy-done | bytes 2097176
  2.2 0.0 copy-start.1
  2.2 1.0 %copy-done.1 = f32[4,32,1024]{2,1,0:T(8,128)S(1)} copy-done((f32[4,32,1024]{2,1,0:T(8,128)S(1)}, f32[4,32,1024]{2,1,0:T(8,128)}, u32[]{:S(2)}) %copy-start.1) | copy-done | bytes 524312
  3.3 0.0 copy-start.2
  3.3 0.9 %copy-done.2 = bf16[4,32,1024]{2,1,0:T(8,128)(2,1)S(1)} copy-done((bf16[4,32,1024]{2,1,0:T(8,128)(2,1)S(1)}, bf16[4,32,1024]{2,1,0:T(8,128)(2,1)}, u32[]{:S(2)}) %copy-start.2) | copy-done | bytes 262168
  4.2 0.0 copy-start.3
  4.2 0.7 %copy-done.3 = s32[4,4,32]{2,1,0:T(4,128)S(1)} copy-done((s32[4,4,32]{2,1,0:T(4,128)S(1)}, s32[4,4,32]{2,1,0:T(4,128)}, u32[]{:S(2)}) %copy-start.3) | copy-done | bytes 2072
  4.9 51.4 %splat.1 = (f32[4,32,1024]{2,1,0:T(8,128)S(1)}, f32[3,4,32,1024]{3,2,1,0:T(8,128)S(1)}) custom-call(s32[4,4,32]{2,1,0:T(4,128)S(1)} %copy-done.3, bf16[4,32,1024]{2,1,0:T(8,128)(2,1)S(1)} %copy-done.2, f32[4,4,32,1024]{3,2,1,0:T(8,128)S(1)} %copy-done, f32[4,32,1024]{2,1,0:T(8,128)S(1)} %copy-done.1), custom_call_target="tpu_custom_call" | custom-call | tf_op jit(solution)/shard_map/splat/pallas_call | solution.py:364
  56.3 1.3 %broadcast_multiply_fusion = f32[3,4,32,1024]{3,2,1,0:T(8,128)} fusion(f32[3,4,32,1024]{3,2,1,0:T(8,128)S(1)} %get-tuple-element.5, f32[4,32,1024]{2,1,0:T(8,128)S(1)} %get-tuple-element.4), kind=kLoop, calls=%fused_computation | loop fusion | flops 393216 | bytes 3670016 | tf_op jit(solution)/shard_map/mul | solution.py:403
  57.6 0.7 %convert_element_type.3 = bf16[4,32,1024]{2,1,0:T(8,128)(2,1)} convert(f32[4,32,1024]{2,1,0:T(8,128)S(1)} %get-tuple-element.4) | non-fusion elementwise | flops 131072 | bytes 786432 | tf_op jit(solution)/shard_map/convert_element_type | solution.py:403
Async XLA Ops:
  0.6 1.6 %copy-start = (f32[4,4,32,1024]{3,2,1,0:T(8,128)S(1)}, f32[4,4,32,1024]{3,2,1,0:T(8,128)}, u32[]{:S(2)}) copy-start(f32[4,4,32,1024]{3,2,1,0:T(8,128)} %frac_ref.1) | copy-start | bytes 6291460
  2.2 1.0 %copy-start.1 = (f32[4,32,1024]{2,1,0:T(8,128)S(1)}, f32[4,32,1024]{2,1,0:T(8,128)}, u32[]{:S(2)}) copy-start(f32[4,32,1024]{2,1,0:T(8,128)} %img_ref.1) | copy-start | bytes 1572868
  3.3 0.9 %copy-start.2 = (bf16[4,32,1024]{2,1,0:T(8,128)(2,1)S(1)}, bf16[4,32,1024]{2,1,0:T(8,128)(2,1)}, u32[]{:S(2)}) copy-start(bf16[4,32,1024]{2,1,0:T(8,128)(2,1)} %adj_ref.1) | copy-start | bytes 786436
  4.2 0.7 %copy-start.3 = (s32[4,4,32]{2,1,0:T(4,128)S(1)}, s32[4,4,32]{2,1,0:T(4,128)}, u32[]{:S(2)}) copy-start(s32[4,4,32]{2,1,0:T(4,128)} %dep_ref.1) | copy-start | bytes 6148

commit v3 on v2

--- a/solution.py
+++ b/solution.py
@@ -10,6 +10,7 @@
 BELOW = 5
 ABOVE = 6
 TILE = 8
+AHEAD = 4
 WIDTH = 256
 MESH = pl.DeviceIdType.MESH
 
@@ -38,6 +39,7 @@
     back_rx,
     img_pad,
     dep_sem,
+    own_dep_sem,
     adj_sem,
     cur_sem,
     fl_sem,
@@ -65,6 +67,7 @@
     chunks = tiles * lanes_parts
     steps = frac_ref.shape[0]
     total = steps * chunks
+    ahead = chunks + chunks * AHEAD // 8
     tall = 2 * rows
     span = BELOW + tall + ABOVE
 
@@ -141,10 +144,11 @@
             pl.semaphore_signal(barrier, inc=1, device_id=where, device_id_type=MESH)
 
     adj_copy = pltpu.make_async_copy(adj_ref, adj_buf, adj_sem)
+    dep_copy = pltpu.make_async_copy(dep_ref, dep_buf.at[y], own_dep_sem)
+    dep_copy.start()
     adj_copy.start()
     lax.fori_loop(0, total, lambda t, z: (frac_local(t).start(), z)[1], 0)
     image_copy.start()
-    dep_buf[y] = dep_ref[...]
     adj_copy.wait()
     for q in range(cols // (2 * TILE)):
         for h in range(2):
@@ -169,11 +173,7 @@
         return z
 
     lax.fori_loop(0, chunks, start_first, 0)
-    lax.fori_loop(chunks, total, lambda t, z: (frac_remote(t, y).start(), z)[1], 0)
-    for send, _, copy in halos:
-        @pl.when(send)
-        def _():
-            copy.start()
+    lax.fori_loop(chunks, ahead, lambda t, z: (frac_remote(t, y).start(), z)[1], 0)
 
     for c in range(chunks):
         cur[c, y] = stage[y, c]
@@ -204,6 +204,7 @@
             by_step = jnp.dot(group, spread, preferred_element_type=jnp.float32)
             land_buf[h, tile] = fixed + h * rows * TILE + by_step.astype(jnp.int32) * TILE
 
+    dep_copy.wait()
     landing(y)
     dep_remote(other).wait_recv()
     landing(other)
@@ -265,6 +266,7 @@
     def first_step(c, z):
         cur_remote(c, other).wait_recv()
         splat(c, c, cur[c])
+        frac_remote(c + ahead, y).start()
         return z
 
     lax.fori_loop(0, chunks, first_step, 0)
@@ -274,7 +276,17 @@
         splat(t, c, combine(t - chunks, c))
         return z
 
-    lax.fori_loop(chunks, total, later_step, 0)
+    def paced_step(t, z):
+        frac_remote(t + ahead, y).start()
+        return later_step(t, z)
+
+    lax.fori_loop(chunks, total - ahead, paced_step, 0)
+    for send, _, copy in halos:
+        @pl.when(send)
+        def _():
+            copy.start()
+
+    lax.fori_loop(total - ahead, total, later_step, 0)
 
     image_copy.wait()
     for index, (_, receive, copy) in enumerate(halos):
@@ -368,7 +380,7 @@
             jax.ShapeDtypeStruct((rows, cols, line), f32),
             jax.ShapeDtypeStruct((3, rows, cols, line), f32),
         ),
-        in_specs=[vmem, hbm, hbm, hbm],
+        in_specs=[hbm, hbm, hbm, hbm],
         out_specs=(vmem, vmem),
         scratch_shapes=[
             pltpu.VMEM((2, steps, rows, cols), jnp.int32),
@@ -387,6 +399,7 @@
             pltpu.VMEM((rows + 2, cols + 2 * TILE, line), f32),
             dma((2,)),
             dma(()),
+            dma(()),
             dma((2, chunks)),
             dma((total,)),
             dma((2, total)),
@@ -399,7 +412,7 @@
         compiler_params=pltpu.CompilerParams(
             collective_id=0, has_side_effects=True, vmem_limit_bytes=40 * 1024 * 1024
         ),
-    )(departure, final_adjoint, fraction, image)
+    )(*(pltpu.with_memory_space_constraint(a, pltpu.HBM) for a in (departure, final_adjoint, fraction, image)))
     return adjoint.astype(jnp.bfloat16), adjoint[None] * gradient
 
 

time: 58.6 us -> 54.4 us (0.928)
  the two profiles are of different devices: /device:TPU:20 before, /device:TPU:16 now
where the time goes in v3:
time: 54.4 us; the launch traced here: 54.2 us
  Pallas kernels  51.5 us (95%)
  other arithmetic  2.12 us (4%)
  between operations  0.64 us (1%)
    pallas_call x1, Pallas kernels, shards(): pl.pallas_call(functools.partial(kernel, slabs, pencils), name='splat', o...  51.5 us
    mul x1, other arithmetic, shards(): return (adjoint.astype(jnp.bfloat16), adjoint[None] * gradient)  1.38 us

profile of v3, /device:TPU:16, one launch (start us, length us, event | category | flops | bytes accessed | tf_op | source)
XLA Modules:
  0.0 54.2 jit_solution(1560377729167553806)
XLA Ops:
  0.6 51.5 %splat.1 = (f32[4,32,1024]{2,1,0:T(8,128)S(1)}, f32[3,4,32,1024]{3,2,1,0:T(8,128)S(1)}) custom-call(s32[4,4,32]{2,1,0:T(4,128)} %dep_ref.1, bf16[4,32,1024]{2,1,0:T(8,128)(2,1)} %adj_ref.1, f32[4,4,32,1024]{3,2,1,0:T(8,128)} %frac_ref.1, f32[4,32,1024]{2,1,0:T(8,128)} %img_ref.1), custom_call_target="tpu_custom_call" | custom-call | tf_op jit(solution)/shard_map/splat/pallas_call | solution.py:376
  52.1 1.4 %broadcast_multiply_fusion = f32[3,4,32,1024]{3,2,1,0:T(8,128)} fusion(f32[3,4,32,1024]{3,2,1,0:T(8,128)S(1)} %get-tuple-element.5, f32[4,32,1024]{2,1,0:T(8,128)S(1)} %get-tuple-element.4), kind=kLoop, calls=%fused_computation | loop fusion | flops 393216 | bytes 3670016 | tf_op jit(solution)/shard_map/mul | solution.py:416
  53.5 0.7 %convert_element_type.3 = bf16[4,32,1024]{2,1,0:T(8,128)(2,1)} convert(f32[4,32,1024]{2,1,0:T(8,128)S(1)} %get-tuple-element.4) | non-fusion elementwise | flops 131072 | bytes 786432 | tf_op jit(solution)/shard_map/convert_element_type | solution.py:416

commit v4 on v3

--- a/solution.py
+++ b/solution.py
@@ -38,6 +38,7 @@
     back_tx,
     back_rx,
     img_pad,
+    relay_buf,
     dep_sem,
     own_dep_sem,
     adj_sem,
@@ -115,13 +116,23 @@
     image_copy = pltpu.make_async_copy(
         img_ref, img_pad.at[pl.ds(1, rows), center_cols], img_sem
     )
+    relay_to = s + 4 * y - 2
+    relay_from = s + 2 - 4 * y
+    outer = s + 2 * y - 1
+    sends_relay = jnp.logical_and(relay_to >= 0, relay_to < slabs)
+    gets_relay = jnp.logical_and(relay_from >= 0, relay_from < slabs)
+    gets_outer = jnp.logical_and(outer >= 0, outer < slabs)
+    relay_copy = remote(
+        img_ref.at[pl.ds(y * (rows - 1), 1)], relay_buf, halo_sem, (0,), {"slab": relay_to}
+    )
+    outer_copy = remote(
+        relay_buf, img_pad.at[pl.ds(other * (rows + 1), 1), center_cols], halo_sem, (1,), {"slab": partner}
+    )
+    inner_copy = remote(
+        img_ref.at[pl.ds(other * (rows - 1), 1)], img_pad.at[pl.ds(y * (rows + 1), 1), center_cols],
+        halo_sem, (4,), {"slab": partner}
+    )
     halos = (
-        (s + 1 < slabs, s >= 1, remote(
-            img_ref.at[pl.ds(rows - 1, 1)], img_pad.at[pl.ds(0, 1), center_cols],
-            halo_sem, (0,), {"slab": s + 1})),
-        (s >= 1, s + 1 < slabs, remote(
-            img_ref.at[pl.ds(0, 1)], img_pad.at[pl.ds(rows + 1, 1), center_cols],
-            halo_sem, (1,), {"slab": s - 1})),
         (p + 1 < pencils, p >= 1, remote(
             img_ref.at[:, pl.ds(cols - TILE, TILE)], img_pad.at[pl.ds(1, rows), pl.ds(0, TILE)],
             halo_sem, (2,), {"pencil": p + 1})),
@@ -132,8 +143,7 @@
 
     barrier = pltpu.get_barrier_semaphore()
     for there, where in (
-        (s >= 1, {"slab": s - 1}),
-        (s + 1 < slabs, {"slab": s + 1}),
+        (slabs > 1, {"slab": partner}),
         (has_lower, {"slab": s - 2}),
         (has_upper, {"slab": s + 2}),
         (p >= 1, {"pencil": p - 1}),
@@ -161,11 +171,15 @@
 
     peers = sum(
         jnp.where(there, 1, 0)
-        for there in (s >= 1, s + 1 < slabs, has_lower, has_upper, p >= 1, p + 1 < pencils)
+        for there in (slabs > 1, has_lower, has_upper, p >= 1, p + 1 < pencils)
     )
     pl.semaphore_wait(barrier, peers)
 
     dep_remote(y).start()
+
+    @pl.when(sends_relay)
+    def _():
+        relay_copy.start()
 
     def start_first(c, z):
         frac_remote(c, y).start()
@@ -173,6 +187,10 @@
         return z
 
     lax.fori_loop(0, chunks, start_first, 0)
+    for send, _, copy in halos:
+        @pl.when(send)
+        def _():
+            copy.start()
     lax.fori_loop(chunks, ahead, lambda t, z: (frac_remote(t, y).start(), z)[1], 0)
 
     for c in range(chunks):
@@ -281,14 +299,26 @@
         return later_step(t, z)
 
     lax.fori_loop(chunks, total - ahead, paced_step, 0)
-    for send, _, copy in halos:
-        @pl.when(send)
-        def _():
-            copy.start()
+    @pl.when(gets_relay)
+    def _():
+        relay_copy.wait_recv()
+        outer_copy.start()
+
+    inner_copy.start()
 
     lax.fori_loop(total - ahead, total, later_step, 0)
 
     image_copy.wait()
+    inner_copy.wait_recv()
+
+    @pl.when(gets_outer)
+    def _():
+        outer_copy.wait_recv()
+
+    @pl.when(jnp.logical_not(gets_outer))
+    def _():
+        img_pad[y * (rows + 1), TILE : TILE + cols] = jnp.zeros((cols, line), jnp.float32)
+
     for index, (_, receive, copy) in enumerate(halos):
         @pl.when(receive)
         def _():
@@ -296,12 +326,8 @@
 
         @pl.when(jnp.logical_not(receive))
         def _():
-            if index < 2:
-                edge = 0 if index == 0 else rows + 1
-                img_pad[edge, TILE : TILE + cols] = jnp.zeros((cols, line), jnp.float32)
-            else:
-                edge = 0 if index == 2 else cols + TILE
-                img_pad[1 : rows + 1, edge : edge + TILE] = jnp.zeros((rows, TILE, line), jnp.float32)
+            edge = 0 if index == 0 else cols + TILE
+            img_pad[1 : rows + 1, edge : edge + TILE] = jnp.zeros((rows, TILE, line), jnp.float32)
 
     lane = lax.broadcasted_iota(jnp.int32, (cols, line), 1)
 
@@ -352,6 +378,16 @@
         return z
 
     lax.fori_loop(0, total, drain, 0)
+    inner_copy.wait_send()
+
+    @pl.when(sends_relay)
+    def _():
+        relay_copy.wait_send()
+
+    @pl.when(gets_relay)
+    def _():
+        outer_copy.wait_send()
+
     for send, _, copy in halos:
         @pl.when(send)
         def _():
@@ -397,6 +433,7 @@
             pltpu.VMEM((chunks, rows, TILE, width), f32),
             pltpu.VMEM((chunks, rows, TILE, width), f32),
             pltpu.VMEM((rows + 2, cols + 2 * TILE, line), f32),
+            pltpu.VMEM((1, cols, line), f32),
             dma((2,)),
             dma(()),
             dma(()),
@@ -407,7 +444,7 @@
             dma((2, total)),
             dma((2, chunks)),
             dma(()),
-            dma((2, 4)),
+            dma((2, 5)),
         ],
         compiler_params=pltpu.CompilerParams(
             collective_id=0, has_side_effects=True, vmem_limit_bytes=40 * 1024 * 1024

time: 54.4 us -> 52.3 us (0.961)
  the two profiles are of different devices: /device:TPU:16 before, /device:TPU:20 now
where the time goes in v4:
time: 52.3 us; the launch traced here: 51.4 us
  Pallas kernels  48.7 us (93%)
  other arithmetic  2.12 us (4%)
  between operations  0.64 us (1%)
    pallas_call x1, Pallas kernels, shards(): pl.pallas_call(functools.partial(kernel, slabs, pencils), name='splat', o...  48.7 us
    mul x1, other arithmetic, shards(): return (adjoint.astype(jnp.bfloat16), adjoint[None] * gradient)  1.38 us

profile of v4, /device:TPU:20, one launch (start us, length us, event | category | flops | bytes accessed | tf_op | source)
XLA Modules:
  0.0 51.4 jit_solution(16150648436423414183)
XLA Ops:
  0.6 48.7 %splat.1 = (f32[4,32,1024]{2,1,0:T(8,128)S(1)}, f32[3,4,32,1024]{3,2,1,0:T(8,128)S(1)}) custom-call(s32[4,4,32]{2,1,0:T(4,128)} %dep_ref.1, bf16[4,32,1024]{2,1,0:T(8,128)(2,1)} %adj_ref.1, f32[4,4,32,1024]{3,2,1,0:T(8,128)} %frac_ref.1, f32[4,32,1024]{2,1,0:T(8,128)} %img_ref.1), custom_call_target="tpu_custom_call" | custom-call | tf_op jit(solution)/shard_map/splat/pallas_call | solution.py:412
  49.3 1.4 %broadcast_multiply_fusion = f32[3,4,32,1024]{3,2,1,0:T(8,128)} fusion(f32[3,4,32,1024]{3,2,1,0:T(8,128)S(1)} %get-tuple-element.5, f32[4,32,1024]{2,1,0:T(8,128)S(1)} %get-tuple-element.4), kind=kLoop, calls=%fused_computation | loop fusion | flops 393216 | bytes 3670016 | tf_op jit(solution)/shard_map/mul | solution.py:453
  50.7 0.7 %convert_element_type.3 = bf16[4,32,1024]{2,1,0:T(8,128)(2,1)} convert(f32[4,32,1024]{2,1,0:T(8,128)S(1)} %get-tuple-element.4) | non-fusion elementwise | flops 131072 | bytes 786432 | tf_op jit(solution)/shard_map/convert_element_type | solution.py:453

commit v5 on v4

--- a/solution.py
+++ b/solution.py
@@ -11,7 +11,7 @@
 ABOVE = 6
 TILE = 8
 AHEAD = 4
-WIDTH = 256
+WIDTH = 512
 MESH = pl.DeviceIdType.MESH
 
 
@@ -349,7 +349,9 @@
         acc[c] = combine_out.reshape(tall, TILE, width)
         back_tx[c] = acc[c, pl.ds(other * rows, rows)]
         back_copy(c).start()
-        adj_out[(slice(None),) + place(c, y)] = acc[c, pl.ds(y * rows, rows)]
+        mine = acc[c, pl.ds(y * rows, rows)]
+        adj_out[(slice(None),) + place(c, y)] = mine
+        grad_out[(slice(None), slice(None)) + place(c, y)] *= mine[None]
         return z
 
     lax.fori_loop(0, chunks, finish, 0)
@@ -357,6 +359,7 @@
     def collect(c, z):
         back_copy(c).wait_recv()
         adj_out[(slice(None),) + place(c, other)] = back_rx[c]
+        grad_out[(slice(None), slice(None)) + place(c, other)] *= back_rx[c][None]
         return z
 
     lax.fori_loop(0, chunks, collect, 0)
@@ -450,7 +453,7 @@
             collective_id=0, has_side_effects=True, vmem_limit_bytes=40 * 1024 * 1024
         ),
     )(*(pltpu.with_memory_space_constraint(a, pltpu.HBM) for a in (departure, final_adjoint, fraction, image)))
-    return adjoint.astype(jnp.bfloat16), adjoint[None] * gradient
+    return adjoint.astype(jnp.bfloat16), gradient
 
 
 def solution(mesh):

time: 52.3 us -> 51.4 us (0.983); the launches traced: 51.4 us -> 51.3 us
  other arithmetic: 2.12 us -> 0.74 us
  local copies, waits for them, and re-layouts: 0 us -> 1.14 us
    mul x1 -> x0, other arithmetic: 1.38 us -> none  [shards(): return (adjoint.astype(jnp.bfloat16), adjoint[None] * gradient)]
    unnamed x0 -> x1, local copies, waits for them, and re-layouts: none -> 1.14 us
where the time goes in v5:
time: 51.4 us; the launch traced here: 51.3 us
  Pallas kernels  48.7 us (95%)
  local copies, waits for them, and re-layouts  1.14 us (2%)
  other arithmetic  0.74 us (1%)
  between operations  0.64 us (1%)
    pallas_call x1, Pallas kernels, shards(): pl.pallas_call(functools.partial(kernel, slabs, pencils), name='splat', o...  48.7 us
    unnamed x1, local copies, waits for them, and re-layouts  1.14 us

profile of v5, /device:TPU:20, one launch (start us, length us, event | category | flops | bytes accessed | tf_op | source)
XLA Modules:
  0.0 51.3 jit_solution(15928834370020506503)
XLA Ops:
  0.6 48.7 %splat.1 = (f32[4,32,1024]{2,1,0:T(8,128)S(1)}, f32[3,4,32,1024]{3,2,1,0:T(8,128)S(1)}) custom-call(s32[4,4,32]{2,1,0:T(4,128)} %dep_ref.1, bf16[4,32,1024]{2,1,0:T(8,128)(2,1)} %adj_ref.1, f32[4,4,32,1024]{3,2,1,0:T(8,128)} %frac_ref.1, f32[4,32,1024]{2,1,0:T(8,128)} %img_ref.1), custom_call_target="tpu_custom_call" | custom-call | tf_op jit(solution)/shard_map/splat/pallas_call | solution.py:415
  49.4 0.7 %convert_element_type.3 = bf16[4,32,1024]{2,1,0:T(8,128)(2,1)} convert(f32[4,32,1024]{2,1,0:T(8,128)S(1)} %get-tuple-element.4) | non-fusion elementwise | flops 131072 | bytes 786432 | tf_op jit(solution)/shard_map/convert_element_type | solution.py:456
  50.1 1.1 %copy.7 = f32[3,4,32,1024]{3,2,1,0:T(8,128)} copy(f32[3,4,32,1024]{3,2,1,0:T(8,128)S(1)} %get-tuple-element.9) | data formatting | bytes 3145728
